TPU v7x, 256 devices: a whole 4x4x8 slice. The times are simulated.
256 devices in a mesh: sub: 4 (over x), row: 16 (over z, core), col: 4 (over y).
Axes of the slice: x: 4, y: 4, z: 8, core: 2. Of those that a mesh axis runs over, the one named last changes fastest.
Arguments:
- leaf_rhs: bfloat16 [4, 64, 4, 64, 256], P('sub', 'row', 'col'), may hold values from -6 to 6
- leaf_inverse: bfloat16 [4, 64, 4, 256, 256], P('sub', 'row', 'col'), may hold values from -0.5 to 0.5
- coupling: bfloat16 [4, 16, 64, 4, 256, 256], P('sub', 'row', None, 'col'), may hold values from -0.01171875 to 0.01171875
- pattern: int32 [4, 16, 64, 4], P('sub', 'row', None, 'col'), may hold values 0 or 1
- top_rhs: bfloat16 [16, 64, 256], replicated, may hold values from -6 to 6
- top_inverse: bfloat16 [16, 256, 256], replicated, may hold values from -0.5 to 0.5
- top_factor: bfloat16 [16, 16, 256, 256], P('row', 'col'), may hold values from -0.09375 to 0.09375
Outputs:
- leaf_solution: bfloat16 [4, 64, 4, 64, 256], P('sub', 'row', 'col')
- top_solution: bfloat16 [16, 64, 256], P('row')
All inputs are finite; a program needn't handle non-finite values. No bound on the sum of `pattern` on one device may be relied on, other than what follows from the above.
Results may differ from a plain program's by a relative error of at most 0.025.
Values may be sent and summed in bfloat16 or wider, within the bound.
No kernel may reach another device: no remote copies, remote signals or barrier semaphores. Data moves between devices by JAX's collectives and lax.ppermute only.
A program may use at most 128 MiB of HBM per device.

v0:
```python
import jax
import jax.numpy as jnp
from jax import lax
from jax.sharding import PartitionSpec as P


def spread(block, axis, source):
    block = jnp.where(lax.axis_index(axis) == source, block, jnp.zeros_like(block))
    return lax.psum(block, axis)


def local(leaf_rhs, leaf_inverse, coupling, pattern, top_rhs, top_inverse, top_factor):
    own_rhs = leaf_rhs[0, :, 0]
    own_inverse = jnp.tril(leaf_inverse[0, :, 0])
    coupled = coupling[0, :, :, 0]
    weights = pattern[0, :, :, 0].astype(jnp.bfloat16)
    blocks_row = coupled.shape[0]
    rhs_count = own_rhs.shape[1]
    block_size = own_rhs.shape[2]
    total_top = top_rhs.shape[0]
    leaf_forward = jnp.einsum(
        "inb,idb->ind", own_rhs, own_inverse, preferred_element_type=jnp.float32
    ).astype(jnp.bfloat16)
    block_slice = coupled
    weight_slice = weights
    scaled = (
        lax.all_gather(leaf_forward, "row", axis=0, tiled=True)[None]
        * weight_slice[:, :, None, None]
    )
    partial_value = jnp.einsum(
        "ainb,aieb->ane", scaled, block_slice, preferred_element_type=jnp.float32
    )
    updates = lax.psum(partial_value.astype(jnp.bfloat16), ("sub", "col")).astype(jnp.float32)
    row_start = lax.axis_index("row") * blocks_row
    full_row = lax.all_gather(top_factor, "col", axis=1, tiled=True)
    row_ids = row_start + jnp.arange(blocks_row)

    def forward_step(block_id, carried):
        pending, solved = carried
        local_row = jnp.clip(block_id - row_start, 0, blocks_row - 1)
        owner_row = block_id // blocks_row
        residue = (
            top_rhs[block_id].astype(jnp.float32) - updates[local_row] - pending[local_row]
        ).astype(jnp.bfloat16)
        solved_piece = jnp.dot(
            residue, jnp.tril(top_inverse[block_id]).T, preferred_element_type=jnp.float32
        ).astype(jnp.bfloat16)
        solved_piece = spread(solved_piece, "row", owner_row)
        column = lax.dynamic_index_in_dim(full_row, block_id, 1, keepdims=False)
        below = (row_ids > block_id).astype(jnp.float32)
        pending = pending + below[:, None, None] * jnp.einsum(
            "nb,aeb->ane", solved_piece, column, preferred_element_type=jnp.float32
        )
        solved = lax.dynamic_update_index_in_dim(solved, solved_piece, block_id, 0)
        return (pending, solved)

    start_state = (
        jnp.zeros((blocks_row, rhs_count, block_size), jnp.float32),
        jnp.zeros((total_top, rhs_count, block_size), jnp.bfloat16),
    )
    forward_all = lax.fori_loop(0, total_top, forward_step, start_state)[1]

    def backward_step(iteration, solved):
        block_id = total_top - 1 - iteration
        own_rows = lax.dynamic_slice_in_dim(solved, row_start, blocks_row, 0)
        above = (row_ids > block_id).astype(jnp.bfloat16)
        column = lax.dynamic_index_in_dim(full_row, block_id, 1, keepdims=False)
        term = jnp.einsum(
            "ane,aeb->nb",
            own_rows * above[:, None, None],
            column,
            preferred_element_type=jnp.float32,
        )
        summed = lax.psum(term.astype(jnp.bfloat16), "row").astype(jnp.float32)
        residue = (forward_all[block_id].astype(jnp.float32) - summed).astype(jnp.bfloat16)
        solved_piece = jnp.dot(
            residue, jnp.tril(top_inverse[block_id]), preferred_element_type=jnp.float32
        ).astype(jnp.bfloat16)
        return lax.dynamic_update_index_in_dim(solved, solved_piece, block_id, 0)

    solution = lax.fori_loop(
        0, total_top, backward_step, jnp.zeros((total_top, rhs_count, block_size), jnp.bfloat16)
    )
    own_top = lax.dynamic_slice_in_dim(solution, row_start, blocks_row, 0)
    block_slice = coupled
    weight_slice = weights
    scaled = own_top[:, None] * weight_slice[:, :, None, None]
    back_sums = lax.psum_scatter(
        jnp.einsum(
            "aine,aieb->inb", scaled, block_slice, preferred_element_type=jnp.float32
        ).astype(jnp.bfloat16),
        "row",
        scatter_dimension=0,
        tiled=True,
    ).astype(jnp.float32)
    leaf_residue = (leaf_forward.astype(jnp.float32) - back_sums).astype(jnp.bfloat16)
    leaf_result = jnp.einsum(
        "inb,ibd->ind", leaf_residue, own_inverse, preferred_element_type=jnp.float32
    ).astype(jnp.bfloat16)
    return (leaf_result[None, :, None], own_top)


def solution(mesh):
    placed = (
        P("sub", "row", "col", None, None),
        P("sub", "row", "col", None, None),
        P("sub", "row", None, "col", None, None),
        P("sub", "row", None, "col"),
        P(),
        P(),
        P("row", "col", None, None),
    )
    return jax.shard_map(
        local,
        mesh=mesh,
        in_specs=placed,
        out_specs=(P("sub", "row", "col", None, None), P("row", None, None)),
        check_vma=False,
    )
```

profile of v0, /device:TPU:4, one launch (start us, length us, event | category | flops | bytes accessed | tf_op | source)
XLA Modules:
  0.0 1736.7 jit_solution(8568360056786855845)
XLA Ops:
  59.8 62.8 %psum.35 = bf16[1,64,256]{2,1,0:T(8,128)(2,1)S(1)} all-reduce(bf16[1,64,256]{2,1,0:T(8,128)(2,1)S(1)} %fusion.62), channel_id=1, replica_groups=mesh['sub'=4,'row'=16,'col'=4] {'sub','col'}, use_global_device_ids=true, to_apply=%region_0.1 | all-reduce | flops 16384 | bytes 65536 | tf_op jit(solution)/shard_map/psum | solution.py:33
  122.7 768.0 %while.34 = (s32[]{:T(128)}, f32[1,64,256]{2,1,0:T(8,128)S(1)}, bf16[16,64,256]{2,1,0:T(8,128)(2,1)S(1)}, s32[1]{0:T(128)}, bf16[1,16,256,256]{3,2,1,0:T(8,128)(...) while((s32[]{:T(128)}, f32[1,64,256]{2,1,0:T(8,128)S(1)}, ...), condition=%wide.region_3.4_spmd.clone, body=%wide.region_1.3_spmd.clone.sunk | while | flops 17088520 | bytes 755900 | solution.py:61
  123.8 45.7 %psum.40 = bf16[64,256]{1,0:T(8,128)(2,1)S(1)} all-reduce(bf16[64,256]{1,0:T(8,128)(2,1)S(1)} %fusion.97), channel_id=1, replica_groups=mesh['sub'=4,'row'=16,'col'=4] {'row'}, use_global_device_ids=true, to_apply=%region_2.2 | all-reduce | flops 16384 | bytes 65536 | tf_op jit(solution)/shard_map/while/body/eval_jaxpr/psum | solution.py:9
  171.8 45.7 %psum.40 = bf16[64,256]{1,0:T(8,128)(2,1)S(1)} all-reduce(bf16[64,256]{1,0:T(8,128)(2,1)S(1)} %fusion.97), channel_id=1, replica_groups=mesh['sub'=4,'row'=16,'col'=4] {'row'}, use_global_device_ids=true, to_apply=%region_2.2 | all-reduce | flops 16384 | bytes 65536 | tf_op jit(solution)/shard_map/while/body/eval_jaxpr/psum | solution.py:9
  219.8 45.7 %psum.40 = bf16[64,256]{1,0:T(8,128)(2,1)S(1)} all-reduce(bf16[64,256]{1,0:T(8,128)(2,1)S(1)} %fusion.97), channel_id=1, replica_groups=mesh['sub'=4,'row'=16,'col'=4] {'row'}, use_global_device_ids=true, to_apply=%region_2.2 | all-reduce | flops 16384 | bytes 65536 | tf_op jit(solution)/shard_map/while/body/eval_jaxpr/psum | solution.py:9
  267.8 45.7 %psum.40 = bf16[64,256]{1,0:T(8,128)(2,1)S(1)} all-reduce(bf16[64,256]{1,0:T(8,128)(2,1)S(1)} %fusion.97), channel_id=1, replica_groups=mesh['sub'=4,'row'=16,'col'=4] {'row'}, use_global_device_ids=true, to_apply=%region_2.2 | all-reduce | flops 16384 | bytes 65536 | tf_op jit(solution)/shard_map/while/body/eval_jaxpr/psum | solution.py:9
  315.8 45.7 %psum.40 = bf16[64,256]{1,0:T(8,128)(2,1)S(1)} all-reduce(bf16[64,256]{1,0:T(8,128)(2,1)S(1)} %fusion.97), channel_id=1, replica_groups=mesh['sub'=4,'row'=16,'col'=4] {'row'}, use_global_device_ids=true, to_apply=%region_2.2 | all-reduce | flops 16384 | bytes 65536 | tf_op jit(solution)/shard_map/while/body/eval_jaxpr/psum | solution.py:9
  363.8 45.7 %psum.40 = bf16[64,256]{1,0:T(8,128)(2,1)S(1)} all-reduce(bf16[64,256]{1,0:T(8,128)(2,1)S(1)} %fusion.97), channel_id=1, replica_groups=mesh['sub'=4,'row'=16,'col'=4] {'row'}, use_global_device_ids=true, to_apply=%region_2.2 | all-reduce | flops 16384 | bytes 65536 | tf_op jit(solution)/shard_map/while/body/eval_jaxpr/psum | solution.py:9
  411.8 45.7 %psum.40 = bf16[64,256]{1,0:T(8,128)(2,1)S(1)} all-reduce(bf16[64,256]{1,0:T(8,128)(2,1)S(1)} %fusion.97), channel_id=1, replica_groups=mesh['sub'=4,'row'=16,'col'=4] {'row'}, use_global_device_ids=true, to_apply=%region_2.2 | all-reduce | flops 16384 | bytes 65536 | tf_op jit(solution)/shard_map/while/body/eval_jaxpr/psum | solution.py:9
  459.8 45.7 %psum.40 = bf16[64,256]{1,0:T(8,128)(2,1)S(1)} all-reduce(bf16[64,256]{1,0:T(8,128)(2,1)S(1)} %fusion.97), channel_id=1, replica_groups=mesh['sub'=4,'row'=16,'col'=4] {'row'}, use_global_device_ids=true, to_apply=%region_2.2 | all-reduce | flops 16384 | bytes 65536 | tf_op jit(solution)/shard_map/while/body/eval_jaxpr/psum | solution.py:9
  555.8 45.7 %psum.40 = bf16[64,256]{1,0:T(8,128)(2,1)S(1)} all-reduce(bf16[64,256]{1,0:T(8,128)(2,1)S(1)} %fusion.97), channel_id=1, replica_groups=mesh['sub'=4,'row'=16,'col'=4] {'row'}, use_global_device_ids=true, to_apply=%region_2.2 | all-reduce | flops 16384 | bytes 65536 | tf_op jit(solution)/shard_map/while/body/eval_jaxpr/psum | solution.py:9
  603.8 45.7 %psum.40 = bf16[64,256]{1,0:T(8,128)(2,1)S(1)} all-reduce(bf16[64,256]{1,0:T(8,128)(2,1)S(1)} %fusion.97), channel_id=1, replica_groups=mesh['sub'=4,'row'=16,'col'=4] {'row'}, use_global_device_ids=true, to_apply=%region_2.2 | all-reduce | flops 16384 | bytes 65536 | tf_op jit(solution)/shard_map/while/body/eval_jaxpr/psum | solution.py:9
  699.8 45.7 %psum.40 = bf16[64,256]{1,0:T(8,128)(2,1)S(1)} all-reduce(bf16[64,256]{1,0:T(8,128)(2,1)S(1)} %fusion.97), channel_id=1, replica_groups=mesh['sub'=4,'row'=16,'col'=4] {'row'}, use_global_device_ids=true, to_apply=%region_2.2 | all-reduce | flops 16384 | bytes 65536 | tf_op jit(solution)/shard_map/while/body/eval_jaxpr/psum | solution.py:9
  795.8 45.7 %psum.40 = bf16[64,256]{1,0:T(8,128)(2,1)S(1)} all-reduce(bf16[64,256]{1,0:T(8,128)(2,1)S(1)} %fusion.97), channel_id=1, replica_groups=mesh['sub'=4,'row'=16,'col'=4] {'row'}, use_global_device_ids=true, to_apply=%region_2.2 | all-reduce | flops 16384 | bytes 65536 | tf_op jit(solution)/shard_map/while/body/eval_jaxpr/psum | solution.py:9
  890.7 765.6 %while.33 = (s32[]{:T(128)}, bf16[16,64,256]{2,1,0:T(8,128)(2,1)S(1)}, bf16[16,64,256]{2,1,0:T(8,128)(2,1)S(1)}, s32[]{:T(128)}, s32[1]{0:T(128)}, /*index=5*/bf...) while((s32[]{:T(128)}, ...), condition=%wide.region_6.7_spmd, body=%wide.region_4.6_spmd.sunk | while | flops 17039368 | bytes 494251 | solution.py:81
  891.8 45.7 %psum.39 = bf16[64,256]{1,0:T(8,128)(2,1)S(1)} all-reduce(bf16[64,256]{1,0:T(8,128)(2,1)S(1)} %convolution_convert_fusion.6), channel_id=1, replica_groups=mesh['sub'=4,'row'=16,'col'=4] {'row'}, use_global_device_ids=true, to_apply=%region_5.5 | all-reduce | flops 16384 | bytes 65536 | tf_op jit(solution)/shard_map/while/body/eval_jaxpr/psum | solution.py:74
  939.6 45.7 %psum.39 = bf16[64,256]{1,0:T(8,128)(2,1)S(1)} all-reduce(bf16[64,256]{1,0:T(8,128)(2,1)S(1)} %convolution_convert_fusion.6), channel_id=1, replica_groups=mesh['sub'=4,'row'=16,'col'=4] {'row'}, use_global_device_ids=true, to_apply=%region_5.5 | all-reduce | flops 16384 | bytes 65536 | tf_op jit(solution)/shard_map/while/body/eval_jaxpr/psum | solution.py:74
  987.5 45.7 %psum.39 = bf16[64,256]{1,0:T(8,128)(2,1)S(1)} all-reduce(bf16[64,256]{1,0:T(8,128)(2,1)S(1)} %convolution_convert_fusion.6), channel_id=1, replica_groups=mesh['sub'=4,'row'=16,'col'=4] {'row'}, use_global_device_ids=true, to_apply=%region_5.5 | all-reduce | flops 16384 | bytes 65536 | tf_op jit(solution)/shard_map/while/body/eval_jaxpr/psum | solution.py:74
  1035.3 45.7 %psum.39 = bf16[64,256]{1,0:T(8,128)(2,1)S(1)} all-reduce(bf16[64,256]{1,0:T(8,128)(2,1)S(1)} %convolution_convert_fusion.6), channel_id=1, replica_groups=mesh['sub'=4,'row'=16,'col'=4] {'row'}, use_global_device_ids=true, to_apply=%region_5.5 | all-reduce | flops 16384 | bytes 65536 | tf_op jit(solution)/shard_map/while/body/eval_jaxpr/psum | solution.py:74
  1083.2 45.7 %psum.39 = bf16[64,256]{1,0:T(8,128)(2,1)S(1)} all-reduce(bf16[64,256]{1,0:T(8,128)(2,1)S(1)} %convolution_convert_fusion.6), channel_id=1, replica_groups=mesh['sub'=4,'row'=16,'col'=4] {'row'}, use_global_device_ids=true, to_apply=%region_5.5 | all-reduce | flops 16384 | bytes 65536 | tf_op jit(solution)/shard_map/while/body/eval_jaxpr/psum | solution.py:74
  1131.0 45.7 %psum.39 = bf16[64,256]{1,0:T(8,128)(2,1)S(1)} all-reduce(bf16[64,256]{1,0:T(8,128)(2,1)S(1)} %convolution_convert_fusion.6), channel_id=1, replica_groups=mesh['sub'=4,'row'=16,'col'=4] {'row'}, use_global_device_ids=true, to_apply=%region_5.5 | all-reduce | flops 16384 | bytes 65536 | tf_op jit(solution)/shard_map/while/body/eval_jaxpr/psum | solution.py:74
  1178.9 45.7 %psum.39 = bf16[64,256]{1,0:T(8,128)(2,1)S(1)} all-reduce(bf16[64,256]{1,0:T(8,128)(2,1)S(1)} %convolution_convert_fusion.6), channel_id=1, replica_groups=mesh['sub'=4,'row'=16,'col'=4] {'row'}, use_global_device_ids=true, to_apply=%region_5.5 | all-reduce | flops 16384 | bytes 65536 | tf_op jit(solution)/shard_map/while/body/eval_jaxpr/psum | solution.py:74
  1226.7 45.7 %psum.39 = bf16[64,256]{1,0:T(8,128)(2,1)S(1)} all-reduce(bf16[64,256]{1,0:T(8,128)(2,1)S(1)} %convolution_convert_fusion.6), channel_id=1, replica_groups=mesh['sub'=4,'row'=16,'col'=4] {'row'}, use_global_device_ids=true, to_apply=%region_5.5 | all-reduce | flops 16384 | bytes 65536 | tf_op jit(solution)/shard_map/while/body/eval_jaxpr/psum | solution.py:74
  1274.6 45.7 %psum.39 = bf16[64,256]{1,0:T(8,128)(2,1)S(1)} all-reduce(bf16[64,256]{1,0:T(8,128)(2,1)S(1)} %convolution_convert_fusion.6), channel_id=1, replica_groups=mesh['sub'=4,'row'=16,'col'=4] {'row'}, use_global_device_ids=true, to_apply=%region_5.5 | all-reduce | flops 16384 | bytes 65536 | tf_op jit(solution)/shard_map/while/body/eval_jaxpr/psum | solution.py:74
  1322.4 45.7 %psum.39 = bf16[64,256]{1,0:T(8,128)(2,1)S(1)} all-reduce(bf16[64,256]{1,0:T(8,128)(2,1)S(1)} %convolution_convert_fusion.6), channel_id=1, replica_groups=mesh['sub'=4,'row'=16,'col'=4] {'row'}, use_global_device_ids=true, to_apply=%region_5.5 | all-reduce | flops 16384 | bytes 65536 | tf_op jit(solution)/shard_map/while/body/eval_jaxpr/psum | solution.py:74
  1370.3 45.7 %psum.39 = bf16[64,256]{1,0:T(8,128)(2,1)S(1)} all-reduce(bf16[64,256]{1,0:T(8,128)(2,1)S(1)} %convolution_convert_fusion.6), channel_id=1, replica_groups=mesh['sub'=4,'row'=16,'col'=4] {'row'}, use_global_device_ids=true, to_apply=%region_5.5 | all-reduce | flops 16384 | bytes 65536 | tf_op jit(solution)/shard_map/while/body/eval_jaxpr/psum | solution.py:74
  1418.1 45.7 %psum.39 = bf16[64,256]{1,0:T(8,128)(2,1)S(1)} all-reduce(bf16[64,256]{1,0:T(8,128)(2,1)S(1)} %convolution_convert_fusion.6), channel_id=1, replica_groups=mesh['sub'=4,'row'=16,'col'=4] {'row'}, use_global_device_ids=true, to_apply=%region_5.5 | all-reduce | flops 16384 | bytes 65536 | tf_op jit(solution)/shard_map/while/body/eval_jaxpr/psum | solution.py:74
  1466.0 45.7 %psum.39 = bf16[64,256]{1,0:T(8,128)(2,1)S(1)} all-reduce(bf16[64,256]{1,0:T(8,128)(2,1)S(1)} %convolution_convert_fusion.6), channel_id=1, replica_groups=mesh['sub'=4,'row'=16,'col'=4] {'row'}, use_global_device_ids=true, to_apply=%region_5.5 | all-reduce | flops 16384 | bytes 65536 | tf_op jit(solution)/shard_map/while/body/eval_jaxpr/psum | solution.py:74
  1513.8 45.7 %psum.39 = bf16[64,256]{1,0:T(8,128)(2,1)S(1)} all-reduce(bf16[64,256]{1,0:T(8,128)(2,1)S(1)} %convolution_convert_fusion.6), channel_id=1, replica_groups=mesh['sub'=4,'row'=16,'col'=4] {'row'}, use_global_device_ids=true, to_apply=%region_5.5 | all-reduce | flops 16384 | bytes 65536 | tf_op jit(solution)/shard_map/while/body/eval_jaxpr/psum | solution.py:74
  1561.6 45.7 %psum.39 = bf16[64,256]{1,0:T(8,128)(2,1)S(1)} all-reduce(bf16[64,256]{1,0:T(8,128)(2,1)S(1)} %convolution_convert_fusion.6), channel_id=1, replica_groups=mesh['sub'=4,'row'=16,'col'=4] {'row'}, use_global_device_ids=true, to_apply=%region_5.5 | all-reduce | flops 16384 | bytes 65536 | tf_op jit(solution)/shard_map/while/body/eval_jaxpr/psum | solution.py:74
  1609.5 45.7 %psum.39 = bf16[64,256]{1,0:T(8,128)(2,1)S(1)} all-reduce(bf16[64,256]{1,0:T(8,128)(2,1)S(1)} %convolution_convert_fusion.6), channel_id=1, replica_groups=mesh['sub'=4,'row'=16,'col'=4] {'row'}, use_global_device_ids=true, to_apply=%region_5.5 | all-reduce | flops 16384 | bytes 65536 | tf_op jit(solution)/shard_map/while/body/eval_jaxpr/psum | solution.py:74
  1663.3 65.1 %reduce-scatter.2.cloned.1.call-done = bf16[4,64,256]{2,1,0:T(8,128)(2,1)} async-done(((bf16[64,64,256]{2,1,0:T(8,128)(2,1)}), bf16[4,64,256]{2,1,0:T(8,128)(2,1)}) %reduce-scatter.2.cloned.1.call-update) | async-done | bytes 131088 | tf_op jit(solution)/shard_map/reduce_scatter | solution.py:88
  (110 shorter events, 313.2 us)
Async XLA Ops:
  7.2 0.9 copy-start
  7.2 45.9 %all-gather.5.cloned.1.call-start = ((), (), s32[]{:S(2)}) async-start(), calls=%async_computation.2 | async-start | bytes 2228224 | tf_op jit(solution)/shard_map/all_gather | solution.py:27
  10.1 112.6 %all-gather.3.cloned.1.call-start = ((), (), s32[]{:S(2)}) async-start(), calls=%async_computation.1 | async-start | bytes 2621440 | tf_op jit(solution)/shard_map/all_gather | solution.py:35
  10.8 1717.5 %reduce-scatter.2.cloned.1.call-start = ((), (), s32[]{:S(2)}) async-start(), calls=%async_computation.3 | async-start | bytes 2228224 | tf_op jit(solution)/shard_map/reduce_scatter | solution.py:88
  1662.7 65.7 %copy-start.1 = (bf16[4,64,256]{2,1,0:T(8,128)(2,1)S(1)}, bf16[4,64,256]{2,1,0:T(8,128)(2,1)}, u32[]{:S(2)}) copy-start(bf16[4,64,256]{2,1,0:T(8,128)(2,1)} %fusion.50) | copy-start | bytes 393220
  1662.7 65.7 %copy-start.2 = (bf16[1,4,1,256,256]{4,3,2,1,0:T(8,128)(2,1)S(1)}, bf16[1,4,1,256,256]{4,3,2,1,0:T(8,128)(2,1)}, u32[]{:S(2)}) copy-start(bf16[1,4,1,256,256]{4,3,2,1,0:T(8,128)(2,1)} %param.12) | copy-start | bytes 1572868
Sparse Core Ops, SparseCore 0:
  10.4 42.6 all-gather.4
  54.9 32.1 all-gather.2
  1662.8 65.5 reduce-scatter.1
where the time goes:
time: 1740 us
  blocking collectives  1530 us (88%)
  waiting for transfers between devices  107 us (6%)
  matrix products  85.4 us (5%)
    psum x16, blocking collectives, backward_step(): summed = lax.psum(term.astype(jnp.bfloat16), 'row').astype(jnp.float32)  732 us
    psum x16, blocking collectives, spread(): return lax.psum(block, axis)  732 us
    reduce_scatter x1, waiting for transfers between devices, local(): lax.psum_scatter(jnp.einsum('aine,aieb->inb', scaled, block_slice, prefer...  65.1 us
    psum x1, blocking collectives, local(): lax.psum(partial_value.astype(jnp.bfloat16), ('sub', 'col'))  62.8 us
    all_gather x1, waiting for transfers between devices, local(): lax.all_gather(leaf_forward, 'row', axis=0, tiled=True)[None]  41.5 us
  transfers between devices with their start and end apart: 3, of which 2 were waited for; matrix products, arithmetic and copies ran while one was open for 0% of the time, Pallas kernels for 0%

commit v1 on v0

--- a/solution.py
+++ b/solution.py
@@ -6,7 +6,7 @@
 
 def spread(block, axis, source):
     block = jnp.where(lax.axis_index(axis) == source, block, jnp.zeros_like(block))
-    return lax.psum(block, axis)
+    return jnp.sum(lax.all_gather(block, axis), axis=0)
 
 
 def local(leaf_rhs, leaf_inverse, coupling, pattern, top_rhs, top_inverse, top_factor):

time: 1740 us -> 1280 us (0.74)
  blocking collectives: 1530 us -> 1060 us
    psum x16 -> x0, blocking collectives: 732 us -> none  [spread(): return lax.psum(block, axis)]
    all_gather x0 -> x16, blocking collectives: none -> 265 us  [spread(): return jnp.sum(lax.all_gather(block, axis), axis=0)]
  transfers between devices with their start and end apart: 3 -> 3, of which waited for: 2 -> 2; matrix products, arithmetic and copies ran while one was open for 0% -> 1% of each run, Pallas kernels for 0% -> 0%
where the time goes in v1:
time: 1280 us; the launch traced here: 1270 us
  blocking collectives  1060 us (83%)
  waiting for transfers between devices  108 us (8%)
  matrix products  85.5 us (7%)
  between operations  13.8 us (1%)
    psum x16, blocking collectives, backward_step(): summed = lax.psum(term.astype(jnp.bfloat16), 'row').astype(jnp.float32)  733 us
    all_gather x16, blocking collectives, spread(): return jnp.sum(lax.all_gather(block, axis), axis=0)  265 us
    reduce_scatter x1, waiting for transfers between devices, local(): lax.psum_scatter(jnp.einsum('aine,aieb->inb', scaled, block_slice, prefer...  65.3 us
    psum x1, blocking collectives, local(): lax.psum(partial_value.astype(jnp.bfloat16), ('sub', 'col'))  62.8 us
    all_gather x1, waiting for transfers between devices, local(): lax.all_gather(leaf_forward, 'row', axis=0, tiled=True)[None]  41.5 us
  transfers between devices with their start and end apart: 3, of which 2 were waited for; matrix products, arithmetic and copies ran while one was open for 1% of the time, Pallas kernels for 0%

profile of v1, /device:TPU:4, one launch (start us, length us, event | category | flops | bytes accessed | tf_op | source)
XLA Modules:
  0.0 1273.4 jit_solution(9164382989859401286)
XLA Ops:
  11.6 41.5 %all-gather.9.cloned.1.call-done = bf16[64,64,256]{2,1,0:T(8,128)(2,1)} async-done(((bf16[4,64,256]{2,1,0:T(8,128)(2,1)}), bf16[64,64,256]{2,1,0:T(8,128)(2,1)}) %all-gather.9.cloned.1.call-update) | async-done | bytes 2097168 | tf_op jit(solution)/shard_map/all_gather | solution.py:27
  59.8 62.8 %psum.21 = bf16[1,64,256]{2,1,0:T(8,128)(2,1)S(1)} all-reduce(bf16[1,64,256]{2,1,0:T(8,128)(2,1)S(1)} %fusion.62), channel_id=1, replica_groups=mesh['sub'=4,'row'=16,'col'=4] {'sub','col'}, use_global_device_ids=true, to_apply=%region_0.1 | all-reduce | flops 16384 | bytes 65536 | tf_op jit(solution)/shard_map/psum | solution.py:33
  122.7 303.0 %while.34 = (s32[]{:T(128)}, f32[1,64,256]{2,1,0:T(8,128)S(1)}, bf16[16,64,256]{2,1,0:T(8,128)(2,1)S(1)}, s32[1]{0:T(128)}, bf16[1,16,256,256]{3,2,1,0:T(8,128)(...) while((s32[]{:T(128)}, f32[1,64,256]{2,1,0:T(8,128)S(1)}, ...), condition=%wide.region_3.4_spmd.clone, body=%wide.region_1.3_spmd.clone.sunk | while | flops 17317896 | bytes 1804486 | solution.py:61
  123.8 17.1 %all-gather.3 = bf16[1024,256]{1,0:T(8,128)(2,1)S(1)} all-gather(bf16[64,256]{1,0:T(8,128)(2,1)S(1)} %fusion.97), channel_id=2, replica_groups=mesh['sub'=4,'row'=16,'col'=4] {'row'}, dimensions={0}, use_global_device_ids=true | all-gather | bytes 557056 | tf_op jit(solution)/shard_map/while/body/eval_jaxpr/all_gather | solution.py:9
  143.3 16.0 %all-gather.3 = bf16[1024,256]{1,0:T(8,128)(2,1)S(1)} all-gather(bf16[64,256]{1,0:T(8,128)(2,1)S(1)} %fusion.97), channel_id=2, replica_groups=mesh['sub'=4,'row'=16,'col'=4] {'row'}, dimensions={0}, use_global_device_ids=true | all-gather | bytes 557056 | tf_op jit(solution)/shard_map/while/body/eval_jaxpr/all_gather | solution.py:9
  161.7 17.5 %all-gather.3 = bf16[1024,256]{1,0:T(8,128)(2,1)S(1)} all-gather(bf16[64,256]{1,0:T(8,128)(2,1)S(1)} %fusion.97), channel_id=2, replica_groups=mesh['sub'=4,'row'=16,'col'=4] {'row'}, dimensions={0}, use_global_device_ids=true | all-gather | bytes 557056 | tf_op jit(solution)/shard_map/while/body/eval_jaxpr/all_gather | solution.py:9
  199.8 17.2 %all-gather.3 = bf16[1024,256]{1,0:T(8,128)(2,1)S(1)} all-gather(bf16[64,256]{1,0:T(8,128)(2,1)S(1)} %fusion.97), channel_id=2, replica_groups=mesh['sub'=4,'row'=16,'col'=4] {'row'}, dimensions={0}, use_global_device_ids=true | all-gather | bytes 557056 | tf_op jit(solution)/shard_map/while/body/eval_jaxpr/all_gather | solution.py:9
  237.6 17.2 %all-gather.3 = bf16[1024,256]{1,0:T(8,128)(2,1)S(1)} all-gather(bf16[64,256]{1,0:T(8,128)(2,1)S(1)} %fusion.97), channel_id=2, replica_groups=mesh['sub'=4,'row'=16,'col'=4] {'row'}, dimensions={0}, use_global_device_ids=true | all-gather | bytes 557056 | tf_op jit(solution)/shard_map/while/body/eval_jaxpr/all_gather | solution.py:9
  257.2 15.9 %all-gather.3 = bf16[1024,256]{1,0:T(8,128)(2,1)S(1)} all-gather(bf16[64,256]{1,0:T(8,128)(2,1)S(1)} %fusion.97), channel_id=2, replica_groups=mesh['sub'=4,'row'=16,'col'=4] {'row'}, dimensions={0}, use_global_device_ids=true | all-gather | bytes 557056 | tf_op jit(solution)/shard_map/while/body/eval_jaxpr/all_gather | solution.py:9
  275.5 17.2 %all-gather.3 = bf16[1024,256]{1,0:T(8,128)(2,1)S(1)} all-gather(bf16[64,256]{1,0:T(8,128)(2,1)S(1)} %fusion.97), channel_id=2, replica_groups=mesh['sub'=4,'row'=16,'col'=4] {'row'}, dimensions={0}, use_global_device_ids=true | all-gather | bytes 557056 | tf_op jit(solution)/shard_map/while/body/eval_jaxpr/all_gather | solution.py:9
  295.0 15.9 %all-gather.3 = bf16[1024,256]{1,0:T(8,128)(2,1)S(1)} all-gather(bf16[64,256]{1,0:T(8,128)(2,1)S(1)} %fusion.97), channel_id=2, replica_groups=mesh['sub'=4,'row'=16,'col'=4] {'row'}, dimensions={0}, use_global_device_ids=true | all-gather | bytes 557056 | tf_op jit(solution)/shard_map/while/body/eval_jaxpr/all_gather | solution.py:9
  313.3 17.2 %all-gather.3 = bf16[1024,256]{1,0:T(8,128)(2,1)S(1)} all-gather(bf16[64,256]{1,0:T(8,128)(2,1)S(1)} %fusion.97), channel_id=2, replica_groups=mesh['sub'=4,'row'=16,'col'=4] {'row'}, dimensions={0}, use_global_device_ids=true | all-gather | bytes 557056 | tf_op jit(solution)/shard_map/while/body/eval_jaxpr/all_gather | solution.py:9
  351.1 17.2 %all-gather.3 = bf16[1024,256]{1,0:T(8,128)(2,1)S(1)} all-gather(bf16[64,256]{1,0:T(8,128)(2,1)S(1)} %fusion.97), channel_id=2, replica_groups=mesh['sub'=4,'row'=16,'col'=4] {'row'}, dimensions={0}, use_global_device_ids=true | all-gather | bytes 557056 | tf_op jit(solution)/shard_map/while/body/eval_jaxpr/all_gather | solution.py:9
  389.0 17.2 %all-gather.3 = bf16[1024,256]{1,0:T(8,128)(2,1)S(1)} all-gather(bf16[64,256]{1,0:T(8,128)(2,1)S(1)} %fusion.97), channel_id=2, replica_groups=mesh['sub'=4,'row'=16,'col'=4] {'row'}, dimensions={0}, use_global_device_ids=true | all-gather | bytes 557056 | tf_op jit(solution)/shard_map/while/body/eval_jaxpr/all_gather | solution.py:9
  425.8 767.1 %while.33 = (s32[]{:T(128)}, bf16[16,64,256]{2,1,0:T(8,128)(2,1)S(1)}, bf16[16,64,256]{2,1,0:T(8,128)(2,1)S(1)}, s32[]{:T(128)}, s32[1]{0:T(128)}, /*index=5*/bf...) while((s32[]{:T(128)}, ...), condition=%wide.region_6.7_spmd, body=%wide.region_4.6_spmd.sunk | while | flops 17039368 | bytes 494251 | solution.py:81
  426.8 47.2 %psum.23 = bf16[64,256]{1,0:T(8,128)(2,1)S(1)} all-reduce(bf16[64,256]{1,0:T(8,128)(2,1)S(1)} %convolution_convert_fusion.6), channel_id=1, replica_groups=mesh['sub'=4,'row'=16,'col'=4] {'row'}, use_global_device_ids=true, to_apply=%region_5.5 | all-reduce | flops 16384 | bytes 65536 | tf_op jit(solution)/shard_map/while/body/eval_jaxpr/psum | solution.py:74
  476.2 45.7 %psum.23 = bf16[64,256]{1,0:T(8,128)(2,1)S(1)} all-reduce(bf16[64,256]{1,0:T(8,128)(2,1)S(1)} %convolution_convert_fusion.6), channel_id=1, replica_groups=mesh['sub'=4,'row'=16,'col'=4] {'row'}, use_global_device_ids=true, to_apply=%region_5.5 | all-reduce | flops 16384 | bytes 65536 | tf_op jit(solution)/shard_map/while/body/eval_jaxpr/psum | solution.py:74
  524.0 45.7 %psum.23 = bf16[64,256]{1,0:T(8,128)(2,1)S(1)} all-reduce(bf16[64,256]{1,0:T(8,128)(2,1)S(1)} %convolution_convert_fusion.6), channel_id=1, replica_groups=mesh['sub'=4,'row'=16,'col'=4] {'row'}, use_global_device_ids=true, to_apply=%region_5.5 | all-reduce | flops 16384 | bytes 65536 | tf_op jit(solution)/shard_map/while/body/eval_jaxpr/psum | solution.py:74
  571.9 45.7 %psum.23 = bf16[64,256]{1,0:T(8,128)(2,1)S(1)} all-reduce(bf16[64,256]{1,0:T(8,128)(2,1)S(1)} %convolution_convert_fusion.6), channel_id=1, replica_groups=mesh['sub'=4,'row'=16,'col'=4] {'row'}, use_global_device_ids=true, to_apply=%region_5.5 | all-reduce | flops 16384 | bytes 65536 | tf_op jit(solution)/shard_map/while/body/eval_jaxpr/psum | solution.py:74
  619.7 45.7 %psum.23 = bf16[64,256]{1,0:T(8,128)(2,1)S(1)} all-reduce(bf16[64,256]{1,0:T(8,128)(2,1)S(1)} %convolution_convert_fusion.6), channel_id=1, replica_groups=mesh['sub'=4,'row'=16,'col'=4] {'row'}, use_global_device_ids=true, to_apply=%region_5.5 | all-reduce | flops 16384 | bytes 65536 | tf_op jit(solution)/shard_map/while/body/eval_jaxpr/psum | solution.py:74
  667.6 45.7 %psum.23 = bf16[64,256]{1,0:T(8,128)(2,1)S(1)} all-reduce(bf16[64,256]{1,0:T(8,128)(2,1)S(1)} %convolution_convert_fusion.6), channel_id=1, replica_groups=mesh['sub'=4,'row'=16,'col'=4] {'row'}, use_global_device_ids=true, to_apply=%region_5.5 | all-reduce | flops 16384 | bytes 65536 | tf_op jit(solution)/shard_map/while/body/eval_jaxpr/psum | solution.py:74
  715.4 45.7 %psum.23 = bf16[64,256]{1,0:T(8,128)(2,1)S(1)} all-reduce(bf16[64,256]{1,0:T(8,128)(2,1)S(1)} %convolution_convert_fusion.6), channel_id=1, replica_groups=mesh['sub'=4,'row'=16,'col'=4] {'row'}, use_global_device_ids=true, to_apply=%region_5.5 | all-reduce | flops 16384 | bytes 65536 | tf_op jit(solution)/shard_map/while/body/eval_jaxpr/psum | solution.py:74
  763.2 45.7 %psum.23 = bf16[64,256]{1,0:T(8,128)(2,1)S(1)} all-reduce(bf16[64,256]{1,0:T(8,128)(2,1)S(1)} %convolution_convert_fusion.6), channel_id=1, replica_groups=mesh['sub'=4,'row'=16,'col'=4] {'row'}, use_global_device_ids=true, to_apply=%region_5.5 | all-reduce | flops 16384 | bytes 65536 | tf_op jit(solution)/shard_map/while/body/eval_jaxpr/psum | solution.py:74
  811.1 45.7 %psum.23 = bf16[64,256]{1,0:T(8,128)(2,1)S(1)} all-reduce(bf16[64,256]{1,0:T(8,128)(2,1)S(1)} %convolution_convert_fusion.6), channel_id=1, replica_groups=mesh['sub'=4,'row'=16,'col'=4] {'row'}, use_global_device_ids=true, to_apply=%region_5.5 | all-reduce | flops 16384 | bytes 65536 | tf_op jit(solution)/shard_map/while/body/eval_jaxpr/psum | solution.py:74
  858.9 45.7 %psum.23 = bf16[64,256]{1,0:T(8,128)(2,1)S(1)} all-reduce(bf16[64,256]{1,0:T(8,128)(2,1)S(1)} %convolution_convert_fusion.6), channel_id=1, replica_groups=mesh['sub'=4,'row'=16,'col'=4] {'row'}, use_global_device_ids=true, to_apply=%region_5.5 | all-reduce | flops 16384 | bytes 65536 | tf_op jit(solution)/shard_map/while/body/eval_jaxpr/psum | solution.py:74
  906.8 45.7 %psum.23 = bf16[64,256]{1,0:T(8,128)(2,1)S(1)} all-reduce(bf16[64,256]{1,0:T(8,128)(2,1)S(1)} %convolution_convert_fusion.6), channel_id=1, replica_groups=mesh['sub'=4,'row'=16,'col'=4] {'row'}, use_global_device_ids=true, to_apply=%region_5.5 | all-reduce | flops 16384 | bytes 65536 | tf_op jit(solution)/shard_map/while/body/eval_jaxpr/psum | solution.py:74
  954.6 45.7 %psum.23 = bf16[64,256]{1,0:T(8,128)(2,1)S(1)} all-reduce(bf16[64,256]{1,0:T(8,128)(2,1)S(1)} %convolution_convert_fusion.6), channel_id=1, replica_groups=mesh['sub'=4,'row'=16,'col'=4] {'row'}, use_global_device_ids=true, to_apply=%region_5.5 | all-reduce | flops 16384 | bytes 65536 | tf_op jit(solution)/shard_map/while/body/eval_jaxpr/psum | solution.py:74
  1002.5 45.7 %psum.23 = bf16[64,256]{1,0:T(8,128)(2,1)S(1)} all-reduce(bf16[64,256]{1,0:T(8,128)(2,1)S(1)} %convolution_convert_fusion.6), channel_id=1, replica_groups=mesh['sub'=4,'row'=16,'col'=4] {'row'}, use_global_device_ids=true, to_apply=%region_5.5 | all-reduce | flops 16384 | bytes 65536 | tf_op jit(solution)/shard_map/while/body/eval_jaxpr/psum | solution.py:74
  1050.3 45.7 %psum.23 = bf16[64,256]{1,0:T(8,128)(2,1)S(1)} all-reduce(bf16[64,256]{1,0:T(8,128)(2,1)S(1)} %convolution_convert_fusion.6), channel_id=1, replica_groups=mesh['sub'=4,'row'=16,'col'=4] {'row'}, use_global_device_ids=true, to_apply=%region_5.5 | all-reduce | flops 16384 | bytes 65536 | tf_op jit(solution)/shard_map/while/body/eval_jaxpr/psum | solution.py:74
  1098.2 45.7 %psum.23 = bf16[64,256]{1,0:T(8,128)(2,1)S(1)} all-reduce(bf16[64,256]{1,0:T(8,128)(2,1)S(1)} %convolution_convert_fusion.6), channel_id=1, replica_groups=mesh['sub'=4,'row'=16,'col'=4] {'row'}, use_global_device_ids=true, to_apply=%region_5.5 | all-reduce | flops 16384 | bytes 65536 | tf_op jit(solution)/shard_map/while/body/eval_jaxpr/psum | solution.py:74
  1146.0 45.7 %psum.23 = bf16[64,256]{1,0:T(8,128)(2,1)S(1)} all-reduce(bf16[64,256]{1,0:T(8,128)(2,1)S(1)} %convolution_convert_fusion.6), channel_id=1, replica_groups=mesh['sub'=4,'row'=16,'col'=4] {'row'}, use_global_device_ids=true, to_apply=%region_5.5 | all-reduce | flops 16384 | bytes 65536 | tf_op jit(solution)/shard_map/while/body/eval_jaxpr/psum | solution.py:74
  1199.8 65.3 %reduce-scatter.2.cloned.1.call-done = bf16[4,64,256]{2,1,0:T(8,128)(2,1)} async-done(((bf16[64,64,256]{2,1,0:T(8,128)(2,1)}), bf16[4,64,256]{2,1,0:T(8,128)(2,1)}) %reduce-scatter.2.cloned.1.call-update) | async-done | bytes 131088 | tf_op jit(solution)/shard_map/reduce_scatter | solution.py:88
  (126 shorter events, 169.6 us)
Async XLA Ops:
  7.2 0.9 copy-start
  7.2 45.9 %all-gather.9.cloned.1.call-start = ((), (), s32[]{:S(2)}) async-start(), calls=%async_computation.2 | async-start | bytes 2228224 | tf_op jit(solution)/shard_map/all_gather | solution.py:27
  10.1 112.6 %all-gather.7.cloned.1.call-start = ((), (), s32[]{:S(2)}) async-start(), calls=%async_computation.1 | async-start | bytes 2621440 | tf_op jit(solution)/shard_map/all_gather | solution.py:35
  10.8 1254.3 %reduce-scatter.2.cloned.1.call-start = ((), (), s32[]{:S(2)}) async-start(), calls=%async_computation.3 | async-start | bytes 2228224 | tf_op jit(solution)/shard_map/reduce_scatter | solution.py:88
  1199.2 65.9 %copy-start.1 = (bf16[4,64,256]{2,1,0:T(8,128)(2,1)S(1)}, bf16[4,64,256]{2,1,0:T(8,128)(2,1)}, u32[]{:S(2)}) copy-start(bf16[4,64,256]{2,1,0:T(8,128)(2,1)} %fusion.50) | copy-start | bytes 393220
  1199.2 65.9 %copy-start.2 = (bf16[1,4,1,256,256]{4,3,2,1,0:T(8,128)(2,1)S(1)}, bf16[1,4,1,256,256]{4,3,2,1,0:T(8,128)(2,1)}, u32[]{:S(2)}) copy-start(bf16[1,4,1,256,256]{4,3,2,1,0:T(8,128)(2,1)} %param.12) | copy-start | bytes 1572868
Sparse Core Ops, SparseCore 0:
  10.4 42.6 all-gather.8
  54.9 32.1 all-gather.6
  1199.3 65.7 reduce-scatter.1
